TPU v7x, 32 devices: a whole 2x2x4 slice. The times are simulated.
32 devices in a mesh: parts: 2 (over x), blk: 16 (over z, y, core).
Axes of the slice: x: 2, y: 2, z: 4, core: 2. Of those that a mesh axis runs over, the one named last changes fastest.
Arguments:
- queries: bfloat16 [256, 4096], P(('parts', 'blk')), parts along dimension 0, may hold values from -48 to 48
- key_cache: bfloat16 [8192, 512], P(('parts', 'blk')), parts along dimension 0, may hold values from -6 to 6
- value_cache: bfloat16 [8192, 512], P(('parts', 'blk')), parts along dimension 0, may hold values from -6 to 6
- tile_page: int32 [8192], P(('parts', 'blk')), parts along dimension 0, may hold values from 0 to 15, never falling along the last dimension, each value on 1 to 512 neighbouring positions
- row_last: int32 [256], P(('parts', 'blk')), parts along dimension 0, may hold values from 0 to 15, as said below
Outputs:
- attention_out: bfloat16 [256, 4096], P(('parts', 'blk')), parts along dimension 0
There are 2 independent parts, one for each index of `parts`. A program takes and returns all parts, laid end to end along the dimension named above; each array names one. Nothing has to cross between parts.
Inputs may be any that keep to these rules, and one draw needn't show every extreme that they name: tile_page never falls along the tile tokens; every page of 0 to 15 has between 1 and 512 tokens, one exactly 512. row_last never falls along the text rows; the first row sees page 0 only and the last row sees every page.
All inputs are finite; a program needn't handle non-finite values.
Results may differ from a plain program's by a relative error of at most 0.00575.
Values may be sent and summed in bfloat16 or wider, within the bound.
No kernel may reach another device: no remote copies, remote signals or barrier semaphores. Data moves between devices by JAX's collectives and lax.ppermute only.
A program may use at most 64 MiB of HBM per device.

v0:
```python
import functools
import math

import jax
import jax.numpy as jnp
from jax import lax
from jax.experimental import pallas as pl
from jax.experimental.pallas import tpu as pltpu
from jax.sharding import PartitionSpec as P


HEADS = 32
KV_HEADS = 4
GROUP = HEADS // KV_HEADS
HEAD_DIM = 128
WIDTH = HEADS * HEAD_DIM
LANES = 128
SHARE = 4
FAR = -(2.0**100)
EXP2_SCALE = math.log2(math.e) / math.sqrt(HEAD_DIM)


def swapped(block, distance):
    devices = lax.axis_size("blk")
    return lax.ppermute(block, "blk", [(i, i ^ distance) for i in range(devices)])


VMEM_BLOCK = pl.BlockSpec(memory_space=pltpu.VMEM)


HBM_BLOCK = pl.BlockSpec(memory_space=pltpu.MemorySpace.HBM)


def in_hbm(array):
    return pltpu.with_memory_space_constraint(array, pltpu.MemorySpace.HBM)


def limits_kernel(q_ref, last_ref, q_out, last, sems):
    rows = q_ref.shape[0]
    moves = ((last_ref, last), (q_ref, q_out.at[:, :WIDTH]))
    copies = [pltpu.make_async_copy(s, d, sems.at[i]) for i, (s, d) in enumerate(moves)]
    for copy in copies:
        copy.start()
    row = lax.broadcasted_iota(jnp.int32, (rows, LANES), 0)
    lane = lax.broadcasted_iota(jnp.int32, (rows, LANES), 1)
    copies[0].wait()
    seen = functools.reduce(
        jnp.logical_or, [(row == r) & (lane == last[r]) for r in range(rows)]
    )
    q_out[:, WIDTH:] = jnp.where(seen, 1.0, 0.0).astype(jnp.bfloat16)
    copies[1].wait()


def limits_call(queries, row_last):
    rows = queries.shape[0]
    return pl.pallas_call(
        limits_kernel,
        out_shape=jax.ShapeDtypeStruct((rows, WIDTH + LANES), jnp.bfloat16),
        in_specs=[HBM_BLOCK] * 2,
        out_specs=VMEM_BLOCK,
        scratch_shapes=[pltpu.SMEM((rows,), jnp.int32), pltpu.SemaphoreType.DMA((2,))],
        compiler_params=pltpu.CompilerParams(vmem_limit_bytes=8 << 20),
    )(in_hbm(queries), in_hbm(row_last))


def stage_kernel(*refs):
    sources, targets, sems = refs[: len(refs) // 2], refs[len(refs) // 2 : -1], refs[-1]
    copies = [
        pltpu.make_async_copy(source, target, sems.at[i])
        for i, (source, target) in enumerate(zip(sources, targets))
    ]
    for copy in copies:
        copy.start()
    for copy in copies:
        copy.wait()


def stage_call(*arrays):
    return pl.pallas_call(
        stage_kernel,
        out_shape=[jax.ShapeDtypeStruct(a.shape, a.dtype) for a in arrays],
        in_specs=[HBM_BLOCK] * len(arrays),
        out_specs=[VMEM_BLOCK] * len(arrays),
        scratch_shapes=[pltpu.SemaphoreType.DMA((len(arrays),))],
        compiler_params=pltpu.CompilerParams(vmem_limit_bytes=8 << 20),
    )(*map(in_hbm, arrays))


def weights_kernel(n_q, n_kv, *refs):
    q_refs, k_refs = refs[:n_q], refs[n_q : n_q + n_kv]
    page_refs = refs[n_q + n_kv : n_q + 2 * n_kv]
    weight_ref, top_ref = refs[n_q + 2 * n_kv :]
    rows, tokens = q_refs[0].shape[0], k_refs[0].shape[0]
    lane = lax.broadcasted_iota(jnp.int32, (rows, LANES), 1)
    token_lane = lax.broadcasted_iota(jnp.int32, (tokens, LANES), 1).astype(jnp.float32)
    pick = jnp.where(
        lax.broadcasted_iota(jnp.int32, (8, LANES), 0) == 0, 1.0, 0.0
    ).astype(jnp.bfloat16)
    hides = []
    for ref in page_refs:
        pages = jnp.broadcast_to(ref[...], (8, tokens)).astype(jnp.float32)
        column = lax.dot_general(
            pages.astype(jnp.bfloat16),
            pick,
            (((0,), (0,)), ((), ())),
            preferred_element_type=jnp.float32,
        )
        hides.append(jnp.where(column > token_lane, FAR, 0.0).astype(jnp.bfloat16))
    tops = [jnp.zeros((rows, LANES), jnp.float32)] * n_q
    last = [ref[:, WIDTH:].astype(jnp.float32) for ref in q_refs]
    count = n_q * GROUP * rows
    for kv in range(KV_HEADS):
        parts = []
        for i, ref in enumerate(q_refs):
            for g in range(GROUP):
                head = kv * GROUP + g
                q = ref[:, head * HEAD_DIM : (head + 1) * HEAD_DIM].astype(jnp.float32)
                parts.append(jnp.concatenate([q, last[i]], axis=1))
        q_all = jnp.concatenate(parts, axis=0).astype(jnp.bfloat16)
        scores = []
        for ref, hide in zip(k_refs, hides):
            k = ref[:, kv * HEAD_DIM : (kv + 1) * HEAD_DIM]
            scores.append(
                lax.dot_general(
                    q_all,
                    jnp.concatenate([k, hide], axis=1),
                    (((1,), (1,)), ((), ())),
                    preferred_element_type=jnp.float32,
                )
            )
        top = functools.reduce(
            jnp.maximum, [jnp.max(s, axis=1, keepdims=True) for s in scores]
        )
        top = top.astype(jnp.bfloat16).astype(jnp.float32)
        for j, s in enumerate(scores):
            weight_ref[
                kv * count : (kv + 1) * count, j * tokens : (j + 1) * tokens
            ] = jnp.exp2((s - top) * EXP2_SCALE).astype(jnp.bfloat16)
        for i in range(n_q):
            for g in range(GROUP):
                at = slice((i * GROUP + g) * rows, (i * GROUP + g + 1) * rows)
                tops[i] = jnp.where(lane == kv * GROUP + g, top[at], tops[i])
    for i in range(n_q):
        top_ref[i * rows : (i + 1) * rows, :] = tops[i]


def weighted(weight_ref, rows, refs, first, kv):
    tokens = refs[0].shape[0]
    ones = jnp.ones((tokens, LANES), jnp.bfloat16)
    parts = []
    for j, ref in enumerate(refs, first):
        v = jnp.concatenate(
            [ref[:, kv * HEAD_DIM : (kv + 1) * HEAD_DIM], ones], axis=1
        )
        weights = weight_ref[rows, j * tokens : (j + 1) * tokens]
        parts.append(jnp.dot(weights, v, preferred_element_type=jnp.float32))
    return functools.reduce(jnp.add, parts)


def early_kernel(weight_ref, *refs):
    v_refs, sum_ref = refs[:-1], refs[-1]
    count = weight_ref.shape[0] // KV_HEADS
    for kv in range(KV_HEADS):
        rows = slice(kv * count, (kv + 1) * count)
        sum_ref[rows, :] = weighted(weight_ref, rows, v_refs, 0, kv)


def late_kernel(n_q, weight_ref, top_ref, sum_ref, v_ref, *out_refs):
    rows, tokens = out_refs[0].shape[0], v_ref.shape[0]
    block = weight_ref.shape[1] // tokens - 1
    count = n_q * GROUP * rows
    lane = lax.broadcasted_iota(jnp.int32, (rows, LANES), 1)
    stats = [top_ref[i * rows : (i + 1) * rows, :] for i in range(n_q)]
    for kv in range(KV_HEADS):
        span = slice(kv * count, (kv + 1) * count)
        total = sum_ref[span, :] + weighted(weight_ref, span, [v_ref], block, kv)
        for i, ref in enumerate(out_refs):
            for g in range(GROUP):
                head = kv * GROUP + g
                at = slice((i * GROUP + g) * rows, (i * GROUP + g + 1) * rows)
                ref[:, head * HEAD_DIM : (head + 1) * HEAD_DIM] = total[
                    at, :HEAD_DIM
                ].astype(jnp.bfloat16)
                mass = total[at, HEAD_DIM:]
                high = mass.astype(jnp.bfloat16).astype(jnp.float32)
                stats[i] = jnp.where(lane == HEADS + head, high, stats[i])
                stats[i] = jnp.where(lane == 2 * HEADS + head, mass - high, stats[i])
    for stat, ref in zip(stats, out_refs):
        ref[:, WIDTH:] = stat.astype(jnp.bfloat16)


def weights_call(q_blocks, k_blocks, page_blocks):
    n_q, n_kv = len(q_blocks), len(k_blocks)
    rows, tokens = q_blocks[0].shape[0], k_blocks[0].shape[0]
    return pl.pallas_call(
        functools.partial(weights_kernel, n_q, n_kv),
        out_shape=[
            jax.ShapeDtypeStruct((n_q * HEADS * rows, n_kv * tokens), jnp.bfloat16),
            jax.ShapeDtypeStruct((n_q * rows, LANES), jnp.float32),
        ],
        in_specs=[VMEM_BLOCK] * (n_q + 2 * n_kv),
        out_specs=[VMEM_BLOCK] * 2,
        compiler_params=pltpu.CompilerParams(vmem_limit_bytes=24 << 20),
    )(*q_blocks, *k_blocks, *page_blocks)


def early_call(weights, v_blocks):
    return pl.pallas_call(
        early_kernel,
        out_shape=jax.ShapeDtypeStruct((weights.shape[0], 2 * LANES), jnp.float32),
        in_specs=[VMEM_BLOCK] * (1 + len(v_blocks)),
        out_specs=VMEM_BLOCK,
        compiler_params=pltpu.CompilerParams(vmem_limit_bytes=24 << 20),
    )(weights, *v_blocks)


def late_call(weights, tops, sums, v_block, n_q):
    rows = tops.shape[0] // n_q
    return pl.pallas_call(
        functools.partial(late_kernel, n_q),
        out_shape=[jax.ShapeDtypeStruct((rows, WIDTH + LANES), jnp.bfloat16)] * n_q,
        in_specs=[VMEM_BLOCK] * 4,
        out_specs=[VMEM_BLOCK] * n_q,
        compiler_params=pltpu.CompilerParams(vmem_limit_bytes=24 << 20),
    )(weights, tops, sums, v_block)


def stats_of(ref):
    stat = ref[:, WIDTH:].astype(jnp.float32)
    mass = pltpu.roll(stat, LANES - HEADS, 1) + pltpu.roll(stat, LANES - 2 * HEADS, 1)
    return stat, mass


def join_kernel(n, *refs):
    parts, sum_ref, stat_ref = refs[:n], refs[n], refs[n + 1]
    tops, masses = zip(*map(stats_of, parts))
    top = functools.reduce(jnp.maximum, tops)
    factors = [jnp.exp2((t - top) * EXP2_SCALE) for t in tops]
    stat_ref[:, :LANES] = top
    stat_ref[:, LANES:] = functools.reduce(
        jnp.add, [f * m for f, m in zip(factors, masses)]
    )
    for head in range(HEADS):
        at = slice(head * HEAD_DIM, (head + 1) * HEAD_DIM)
        sum_ref[:, at] = functools.reduce(
            jnp.add,
            [
                factor[:, head : head + 1] * ref[:, at].astype(jnp.float32)
                for factor, ref in zip(factors, parts)
            ],
        )


def merge_kernel(sum_ref, stat_ref, part_ref, out_ref):
    top, mass = stat_ref[:, :LANES], stat_ref[:, LANES:]
    part_top, part_mass = stats_of(part_ref)
    best = jnp.maximum(top, part_top)
    factor = jnp.exp2((top - best) * EXP2_SCALE)
    part_factor = jnp.exp2((part_top - best) * EXP2_SCALE)
    total = factor * mass + part_factor * part_mass
    share, part_share = factor / total, part_factor / total
    for head in range(HEADS):
        at = slice(head * HEAD_DIM, (head + 1) * HEAD_DIM)
        part = part_ref[:, at].astype(jnp.float32)
        value = share[:, head : head + 1] * sum_ref[:, at]
        value = value + part_share[:, head : head + 1] * part
        out_ref[:, at] = value.astype(jnp.bfloat16)


def join_call(parts):
    rows = parts[0].shape[0]
    return pl.pallas_call(
        functools.partial(join_kernel, len(parts)),
        out_shape=[
            jax.ShapeDtypeStruct((rows, WIDTH), jnp.float32),
            jax.ShapeDtypeStruct((rows, 2 * LANES), jnp.float32),
        ],
        in_specs=[VMEM_BLOCK] * len(parts),
        out_specs=[VMEM_BLOCK] * 2,
        compiler_params=pltpu.CompilerParams(vmem_limit_bytes=8 << 20),
    )(*parts)


def merge_call(sums, stats, part):
    return pl.pallas_call(
        merge_kernel,
        out_shape=jax.ShapeDtypeStruct(sums.shape, jnp.bfloat16),
        in_specs=[VMEM_BLOCK] * 3,
        out_specs=VMEM_BLOCK,
        compiler_params=pltpu.CompilerParams(vmem_limit_bytes=8 << 20),
    )(sums, stats, part)


def pooled(block, own):
    across = swapped(block, 2)
    beside = swapped(block, 1)
    return [own, beside, across, swapped(across, 1)]


def attend(queries, key_cache, value_cache, tile_page, row_last):
    groups = lax.axis_size("blk") // SHARE
    pages = tile_page.reshape(1, -1)
    own_q = limits_call(queries, row_last)
    own_k, own_v, own_page = stage_call(key_cache, value_cache, pages)
    k_blocks = pooled(key_cache, own_k)
    v_blocks = pooled(value_cache, own_v)
    page_blocks = pooled(pages, own_page)
    q_blocks = [own_q] + [swapped(own_q, SHARE * d) for d in range(1, groups)]
    partials = []
    for start in range(0, groups, 4):
        some = q_blocks[start : start + 4]
        weights, tops = weights_call(some, k_blocks, page_blocks)
        sums = early_call(weights, v_blocks[:-1])
        partials += late_call(weights, tops, sums, v_blocks[-1], len(some))
    parts = [partials[0]] + [swapped(partials[d], SHARE * d) for d in range(1, groups)]
    sums, stats = join_call(parts[:2] + parts[3:])
    return merge_call(sums, stats, parts[2])


def solution(mesh):
    placed = (
        P(("parts", "blk"), None),
        P(("parts", "blk"), None),
        P(("parts", "blk"), None),
        P(("parts", "blk")),
        P(("parts", "blk")),
    )
    return jax.shard_map(
        attend, mesh=mesh, in_specs=placed, out_specs=P(("parts", "blk"), None), check_vma=False
    )
```

profile of v0, /device:TPU:0, one launch (start us, length us, event | category | flops | bytes accessed | tf_op | source)
XLA Modules:
  0.0 51.0 jit_solution(4174596231570579797)
XLA Ops:
  0.0 3.0 %collective-permute-start.4 = (bf16[256,512]{1,0:T(8,128)(2,1)}, bf16[256,512]{1,0:T(8,128)(2,1)S(1)}, u32[]{:S(2)}, u32[]{:S(2)}) collective-permute-start(bf16[256,512]{1,0:T(8,128)(2,1)} %refs_0_.1), channel_id=1, source_target_pairs={{0,2},{1,3},{2,0},{3,1},{4,6},{5,7},{6,4},{7,5},{8,10},{9,11},{10,... | collective-permute-start | bytes 786440 | tf_op jit(solution)/shard_map/ppermute | solution.py:25
  3.0 0.0 collective-permute-start.10
  3.0 0.0 collective-permute-start.3
  3.0 7.3 %collective-permute-done.4.refs_6_ = bf16[256,512]{1,0:T(8,128)(2,1)S(1)} collective-permute-done((bf16[256,512]{1,0:T(8,128)(2,1)}, bf16[256,512]{1,0:T(8,128)(2,1)S(1)}, u32[]{:S(2)}, u32[]{:S(2)}) %collective-permute-start.4) | collective-permute-done | bytes 262176 | tf_op jit(solution)/shard_map/ppermute | solution.py:25
  10.4 0.0 collective-permute-start.5
  10.4 0.5 collective-permute-start.9
  10.9 4.3 %collective-permute-done.10.refs_2_ = bf16[256,512]{1,0:T(8,128)(2,1)S(1)} collective-permute-done((bf16[256,512]{1,0:T(8,128)(2,1)}, bf16[256,512]{1,0:T(8,128)(2,1)S(1)}, u32[]{:S(2)}, u32[]{:S(2)}) %collective-permute-start.10) | collective-permute-done | bytes 262176 | tf_op jit(solution)/shard_map/ppermute | solution.py:25
  15.1 0.0 collective-permute-start.11
  15.1 0.5 collective-permute-start.6
  15.6 1.0 %collective-permute-done.6.refs_9_ = s32[1,256]{1,0:T(1,128)S(1)} collective-permute-done((s32[1,256]{1,0:T(1,128)}, s32[1,256]{1,0:T(1,128)S(1)}, u32[]{:S(2)}, u32[]{:S(2)}) %collective-permute-start.6) | collective-permute-done | bytes 1056 | tf_op jit(solution)/shard_map/ppermute | solution.py:25
  16.7 1.7 %collective-permute-start.7 = (s32[1,256]{1,0:T(1,128)}, s32[1,256]{1,0:T(1,128)S(1)}, u32[]{:S(2)}, u32[]{:S(2)}) collective-permute-start(s32[1,256]{1,0:T(1,128)} %bitcast.2), channel_id=1, source_target_pairs={{0,2},{1,3},{2,0},{3,1},{4,6},{5,7},{6,4},{7,5},{8,10},{9,11},{10,... | collective-permute-start | bytes 3080 | tf_op jit(solution)/shard_map/ppermute | solution.py:25
  18.4 2.0 %collective-permute-done.7.refs_10_ = s32[1,256]{1,0:T(1,128)S(1)} collective-permute-done((s32[1,256]{1,0:T(1,128)}, s32[1,256]{1,0:T(1,128)S(1)}, u32[]{:S(2)}, u32[]{:S(2)}) %collective-permute-start.7) | collective-permute-done | bytes 1056 | tf_op jit(solution)/shard_map/ppermute | solution.py:25
  20.5 0.0 collective-permute-start.8
  20.5 0.9 %shard_map.55.refs_0_ = bf16[8,4224]{1,0:T(8,128)(2,1)S(1)} custom-call(bf16[8,4096]{1,0:T(8,128)(2,1)} %q_ref.1, s32[8]{0:T(128)} %last_ref.1), custom_call_target="tpu_custom_call" | custom-call | tf_op jit(solution)/shard_map/pallas_call | solution.py:56
  21.3 0.3 collective-permute-done.8.refs_11_
  21.6 1.8 %collective-permute-start = (bf16[8,4224]{1,0:T(8,128)(2,1)S(1)}, bf16[8,4224]{1,0:T(8,128)(2,1)S(1)}, u32[]{:S(2)}, u32[]{:S(2)}) collective-permute-start(bf16[8,4224]{1,0:T(8,128)(2,1)S(1)} %shard_map.55.refs_0_), channel_id=1, source_target_pairs={{0,4},{1,5},{2,6},{3,7},{4,0},{5,1},{6,2},{7,3},{8,12},{9,13},{10,... | collective-permute-start | bytes 202760 | tf_op jit(solution)/shard_map/ppermute | solution.py:25
  23.4 2.6 %collective-permute-done.refs_1_ = bf16[8,4224]{1,0:T(8,128)(2,1)S(1)} collective-permute-done((bf16[8,4224]{1,0:T(8,128)(2,1)S(1)}, bf16[8,4224]{1,0:T(8,128)(2,1)S(1)}, u32[]{:S(2)}, u32[]{:S(2)}) %collective-permute-start) | collective-permute-done | bytes 67616 | tf_op jit(solution)/shard_map/ppermute | solution.py:25
  26.0 2.8 %collective-permute-start.1 = (bf16[8,4224]{1,0:T(8,128)(2,1)S(1)}, bf16[8,4224]{1,0:T(8,128)(2,1)S(1)}, u32[]{:S(2)}, u32[]{:S(2)}) collective-permute-start(bf16[8,4224]{1,0:T(8,128)(2,1)S(1)} %shard_map.55.refs_0_), channel_id=1, source_target_pairs={{0,8},{1,9},{2,10},{3,11},{4,12},{5,13},{6,14},{7,15},{8,0},{9,1},... | collective-permute-start | bytes 202760 | tf_op jit(solution)/shard_map/ppermute | solution.py:25
  28.8 2.8 %collective-permute-done.1.refs_2_ = bf16[8,4224]{1,0:T(8,128)(2,1)S(1)} collective-permute-done((bf16[8,4224]{1,0:T(8,128)(2,1)S(1)}, bf16[8,4224]{1,0:T(8,128)(2,1)S(1)}, u32[]{:S(2)}, u32[]{:S(2)}) %collective-permute-start.1) | collective-permute-done | bytes 67616 | tf_op jit(solution)/shard_map/ppermute | solution.py:25
  31.6 4.0 %collective-permute-start.2 = (bf16[8,4224]{1,0:T(8,128)(2,1)S(1)}, bf16[8,4224]{1,0:T(8,128)(2,1)S(1)}, u32[]{:S(2)}, u32[]{:S(2)}) collective-permute-start(bf16[8,4224]{1,0:T(8,128)(2,1)S(1)} %shard_map.55.refs_0_), channel_id=1, source_target_pairs={{0,12},{1,13},{2,14},{3,15},{4,8},{5,9},{6,10},{7,11},{8,4},{9,5},... | collective-permute-start | bytes 202760 | tf_op jit(solution)/shard_map/ppermute | solution.py:25
  35.6 1.1 %shard_map.56 = (bf16[256,512]{1,0:T(8,128)(2,1)S(1)}, bf16[256,512]{1,0:T(8,128)(2,1)S(1)}, s32[1,256]{1,0:T(1,128)S(1)}) custom-call(bf16[256,512]{1,0:T(8,128)(2,1)} %refs_0_.1, bf16[256,512]{1,0:T(8,128)(2,1)} %refs_1_.1, s32[1,256]{1,0:T(1,128)} %bitcast.3), custom_call_target="tpu_custom_call" | custom-call | tf_op jit(solution)/shard_map/pallas_call | solution.py:79
  36.6 1.2 %collective-permute-done.2.refs_3_ = bf16[8,4224]{1,0:T(8,128)(2,1)S(1)} collective-permute-done((bf16[8,4224]{1,0:T(8,128)(2,1)S(1)}, bf16[8,4224]{1,0:T(8,128)(2,1)S(1)}, u32[]{:S(2)}, u32[]{:S(2)}) %collective-permute-start.2) | collective-permute-done | bytes 67616 | tf_op jit(solution)/shard_map/ppermute | solution.py:25
  37.8 0.0 collective-permute-done.3.refs_5_
  37.8 0.0 collective-permute-done.5.refs_7_
  37.8 1.4 %shard_map.57 = (bf16[1024,1024]{1,0:T(8,128)(2,1)S(1)}, f32[32,128]{1,0:T(8,128)S(1)}) custom-call(bf16[8,4224]{1,0:T(8,128)(2,1)S(1)} %shard_map.55.refs_0_, bf16[8,4224]{1,0:T(8,128)(2,1)S(1)} %collective-permute-done.refs_1_, bf16[8,4224]{1,0:T(8,128)(2,1)S(1)} %collective-permute-done.1.refs_2_, bf16[8,4224]{1,0:T(8,128)(2,1)S(1)} %collective-permute-done.2.refs_3_, ...), custom_call_target="tpu_custom_call" | custom-call | tf_op jit(solution)/shard_map/pallas_call | solution.py:195
  39.3 0.0 collective-permute-done.9.refs_1_
  39.3 0.6 %shard_map.58.sum_ref = f32[1024,256]{1,0:T(8,128)S(1)} custom-call(bf16[1024,1024]{1,0:T(8,128)(2,1)S(1)} %get-tuple-element.18.weight_ref, bf16[256,512]{1,0:T(8,128)(2,1)S(1)} %get-tuple-element.20.refs_0_, bf16[256,512]{1,0:T(8,128)(2,1)S(1)} %collective-permute-done.9.refs_1_, bf16[256,512]{1,0:T(8,128)(2,1)S(1)} %collective-permute-done.10.refs_2_), custom_call_target="tpu_custom_call" | custom-call | tf_op jit(solution)/shard_map/pallas_call | solution.py:208
  39.9 0.0 collective-permute-done.11.v_ref
  39.9 0.3 shard_map.59
  40.2 0.1 collective-permute-start.12
  40.3 3.9 %collective-permute-start.13 = (bf16[8,4224]{1,0:T(8,128)(2,1)S(1)}, bf16[8,4224]{1,0:T(8,128)(2,1)S(1)}, u32[]{:S(2)}, u32[]{:S(2)}) collective-permute-start(bf16[8,4224]{1,0:T(8,128)(2,1)S(1)} %get-tuple-element.23), channel_id=1, source_target_pairs={{0,12},{1,13},{2,14},{3,15},{4,8},{5,9},{6,10},{7,11},{8,4},{9,5},... | collective-permute-start | bytes 202760 | tf_op jit(solution)/shard_map/ppermute | solution.py:25
  44.2 0.5 collective-permute-start.14
  44.7 0.0 collective-permute-done.12.refs_1_
  44.7 2.5 %collective-permute-done.13.refs_2_ = bf16[8,4224]{1,0:T(8,128)(2,1)S(1)} collective-permute-done((bf16[8,4224]{1,0:T(8,128)(2,1)S(1)}, bf16[8,4224]{1,0:T(8,128)(2,1)S(1)}, u32[]{:S(2)}, u32[]{:S(2)}) %collective-permute-start.13) | collective-permute-done | bytes 67616 | tf_op jit(solution)/shard_map/ppermute | solution.py:25
  47.2 0.2 shard_map.60
  47.4 2.7 %collective-permute-done.14.part_ref = bf16[8,4224]{1,0:T(8,128)(2,1)S(1)} collective-permute-done((bf16[8,4224]{1,0:T(8,128)(2,1)S(1)}, bf16[8,4224]{1,0:T(8,128)(2,1)S(1)}, u32[]{:S(2)}, u32[]{:S(2)}) %collective-permute-start.14) | collective-permute-done | bytes 67616 | tf_op jit(solution)/shard_map/ppermute | solution.py:25
  50.1 0.9 %shard_map.61 = bf16[8,4096]{1,0:T(8,128)(2,1)} custom-call(f32[8,4096]{1,0:T(8,128)S(1)} %get-tuple-element.24.sum_ref, f32[8,256]{1,0:T(8,128)S(1)} %get-tuple-element.25.stat_ref, bf16[8,4224]{1,0:T(8,128)(2,1)S(1)} %collective-permute-done.14.part_ref), custom_call_target="tpu_custom_call" | custom-call | tf_op jit(solution)/shard_map/pallas_call | solution.py:285
Async XLA Ops:
  0.0 10.4 %collective-permute-start.4 = (bf16[256,512]{1,0:T(8,128)(2,1)}, bf16[256,512]{1,0:T(8,128)(2,1)S(1)}, u32[]{:S(2)}, u32[]{:S(2)}) collective-permute-start(bf16[256,512]{1,0:T(8,128)(2,1)} %refs_0_.1), channel_id=1, source_target_pairs={{0,2},{1,3},{2,0},{3,1},{4,6},{5,7},{6,4},{7,5},{8,10},{9,11},{10,... | collective-permute-start | bytes 786440 | tf_op jit(solution)/shard_map/ppermute | solution.py:25
  3.0 12.1 %collective-permute-start.10 = (bf16[256,512]{1,0:T(8,128)(2,1)}, bf16[256,512]{1,0:T(8,128)(2,1)S(1)}, u32[]{:S(2)}, u32[]{:S(2)}) collective-permute-start(bf16[256,512]{1,0:T(8,128)(2,1)} %refs_1_.1), channel_id=1, source_target_pairs={{0,2},{1,3},{2,0},{3,1},{4,6},{5,7},{6,4},{7,5},{8,10},{9,11},{10,... | collective-permute-start | bytes 786440 | tf_op jit(solution)/shard_map/ppermute | solution.py:25
  3.0 34.8 %collective-permute-start.3 = (bf16[256,512]{1,0:T(8,128)(2,1)}, bf16[256,512]{1,0:T(8,128)(2,1)S(1)}, u32[]{:S(2)}, u32[]{:S(2)}) collective-permute-start(bf16[256,512]{1,0:T(8,128)(2,1)} %refs_0_.1), channel_id=1, source_target_pairs={{0,1},{1,0},{2,3},{3,2},{4,5},{5,4},{6,7},{7,6},{8,9},{9,8},{10,11... | collective-permute-start | bytes 786440 | tf_op jit(solution)/shard_map/ppermute | solution.py:25
  10.4 27.5 %collective-permute-start.5 = (bf16[256,512]{1,0:T(8,128)(2,1)S(1)}, bf16[256,512]{1,0:T(8,128)(2,1)S(1)}, u32[]{:S(2)}, u32[]{:S(2)}) collective-permute-start(bf16[256,512]{1,0:T(8,128)(2,1)S(1)} %collective-permute-done.4.refs_6_), channel_id=1, source_target_pairs={{0,1},{1,0},{2,3},{3,2},{4,5},{5,4},{6,7},{7,6},{8,9},{9,8},{10,11... | collective-permute-start | bytes 786440 | tf_op jit(solution)/shard_map/ppermute | solution.py:25
  10.4 28.9 %collective-permute-start.9 = (bf16[256,512]{1,0:T(8,128)(2,1)}, bf16[256,512]{1,0:T(8,128)(2,1)S(1)}, u32[]{:S(2)}, u32[]{:S(2)}) collective-permute-start(bf16[256,512]{1,0:T(8,128)(2,1)} %refs_1_.1), channel_id=1, source_target_pairs={{0,1},{1,0},{2,3},{3,2},{4,5},{5,4},{6,7},{7,6},{8,9},{9,8},{10,11... | collective-permute-start | bytes 786440 | tf_op jit(solution)/shard_map/ppermute | solution.py:25
  15.1 24.7 %collective-permute-start.11 = (bf16[256,512]{1,0:T(8,128)(2,1)S(1)}, bf16[256,512]{1,0:T(8,128)(2,1)S(1)}, u32[]{:S(2)}, u32[]{:S(2)}) collective-permute-start(bf16[256,512]{1,0:T(8,128)(2,1)S(1)} %collective-permute-done.10.refs_2_), channel_id=1, source_target_pairs={{0,1},{1,0},{2,3},{3,2},{4,5},{5,4},{6,7},{7,6},{8,9},{9,8},{10,11... | collective-permute-start | bytes 786440 | tf_op jit(solution)/shard_map/ppermute | solution.py:25
  15.1 1.5 %collective-permute-start.6 = (s32[1,256]{1,0:T(1,128)}, s32[1,256]{1,0:T(1,128)S(1)}, u32[]{:S(2)}, u32[]{:S(2)}) collective-permute-start(s32[1,256]{1,0:T(1,128)} %bitcast.1), channel_id=1, source_target_pairs={{0,1},{1,0},{2,3},{3,2},{4,5},{5,4},{6,7},{7,6},{8,9},{9,8},{10,11... | collective-permute-start | bytes 3080 | tf_op jit(solution)/shard_map/ppermute | solution.py:25
  16.7 3.8 %collective-permute-start.7 = (s32[1,256]{1,0:T(1,128)}, s32[1,256]{1,0:T(1,128)S(1)}, u32[]{:S(2)}, u32[]{:S(2)}) collective-permute-start(s32[1,256]{1,0:T(1,128)} %bitcast.2), channel_id=1, source_target_pairs={{0,2},{1,3},{2,0},{3,1},{4,6},{5,7},{6,4},{7,5},{8,10},{9,11},{10,... | collective-permute-start | bytes 3080 | tf_op jit(solution)/shard_map/ppermute | solution.py:25
  20.5 1.2 %collective-permute-start.8 = (s32[1,256]{1,0:T(1,128)S(1)}, s32[1,256]{1,0:T(1,128)S(1)}, u32[]{:S(2)}, u32[]{:S(2)}) collective-permute-start(s32[1,256]{1,0:T(1,128)S(1)} %collective-permute-done.7.refs_10_), channel_id=1, source_target_pairs={{0,1},{1,0},{2,3},{3,2},{4,5},{5,4},{6,7},{7,6},{8,9},{9,8},{10,11... | collective-permute-start | bytes 3080 | tf_op jit(solution)/shard_map/ppermute | solution.py:25
  21.6 4.4 %collective-permute-start = (bf16[8,4224]{1,0:T(8,128)(2,1)S(1)}, bf16[8,4224]{1,0:T(8,128)(2,1)S(1)}, u32[]{:S(2)}, u32[]{:S(2)}) collective-permute-start(bf16[8,4224]{1,0:T(8,128)(2,1)S(1)} %shard_map.55.refs_0_), channel_id=1, source_target_pairs={{0,4},{1,5},{2,6},{3,7},{4,0},{5,1},{6,2},{7,3},{8,12},{9,13},{10,... | collective-permute-start | bytes 202760 | tf_op jit(solution)/shard_map/ppermute | solution.py:25
  26.0 5.5 %collective-permute-start.1 = (bf16[8,4224]{1,0:T(8,128)(2,1)S(1)}, bf16[8,4224]{1,0:T(8,128)(2,1)S(1)}, u32[]{:S(2)}, u32[]{:S(2)}) collective-permute-start(bf16[8,4224]{1,0:T(8,128)(2,1)S(1)} %shard_map.55.refs_0_), channel_id=1, source_target_pairs={{0,8},{1,9},{2,10},{3,11},{4,12},{5,13},{6,14},{7,15},{8,0},{9,1},... | collective-permute-start | bytes 202760 | tf_op jit(solution)/shard_map/ppermute | solution.py:25
  31.6 6.3 %collective-permute-start.2 = (bf16[8,4224]{1,0:T(8,128)(2,1)S(1)}, bf16[8,4224]{1,0:T(8,128)(2,1)S(1)}, u32[]{:S(2)}, u32[]{:S(2)}) collective-permute-start(bf16[8,4224]{1,0:T(8,128)(2,1)S(1)} %shard_map.55.refs_0_), channel_id=1, source_target_pairs={{0,12},{1,13},{2,14},{3,15},{4,8},{5,9},{6,10},{7,11},{8,4},{9,5},... | collective-permute-start | bytes 202760 | tf_op jit(solution)/shard_map/ppermute | solution.py:25
  40.2 4.4 %collective-permute-start.12 = (bf16[8,4224]{1,0:T(8,128)(2,1)S(1)}, bf16[8,4224]{1,0:T(8,128)(2,1)S(1)}, u32[]{:S(2)}, u32[]{:S(2)}) collective-permute-start(bf16[8,4224]{1,0:T(8,128)(2,1)S(1)} %get-tuple-element.22), channel_id=1, source_target_pairs={{0,4},{1,5},{2,6},{3,7},{4,0},{5,1},{6,2},{7,3},{8,12},{9,13},{10,... | collective-permute-start | bytes 202760 | tf_op jit(solution)/shard_map/ppermute | solution.py:25
  40.3 6.9 %collective-permute-start.13 = (bf16[8,4224]{1,0:T(8,128)(2,1)S(1)}, bf16[8,4224]{1,0:T(8,128)(2,1)S(1)}, u32[]{:S(2)}, u32[]{:S(2)}) collective-permute-start(bf16[8,4224]{1,0:T(8,128)(2,1)S(1)} %get-tuple-element.23), channel_id=1, source_target_pairs={{0,12},{1,13},{2,14},{3,15},{4,8},{5,9},{6,10},{7,11},{8,4},{9,5},... | collective-permute-start | bytes 202760 | tf_op jit(solution)/shard_map/ppermute | solution.py:25
  44.2 5.9 %collective-permute-start.14 = (bf16[8,4224]{1,0:T(8,128)(2,1)S(1)}, bf16[8,4224]{1,0:T(8,128)(2,1)S(1)}, u32[]{:S(2)}, u32[]{:S(2)}) collective-permute-start(bf16[8,4224]{1,0:T(8,128)(2,1)S(1)} %get-tuple-element.26), channel_id=1, source_target_pairs={{0,8},{1,9},{2,10},{3,11},{4,12},{5,13},{6,14},{7,15},{8,0},{9,1},... | collective-permute-start | bytes 202760 | tf_op jit(solution)/shard_map/ppermute | solution.py:25
where the time goes:
time: 51.1 us; the launch traced here: 51 us
  waiting for transfers between devices  26.7 us (52%)
  starting transfers between devices  18.8 us (37%)
  Pallas kernels  5.36 us (10%)
    ppermute x15, waiting for transfers between devices, swapped(): lax.ppermute(block, 'blk', [(i, i ^ distance) for i in range(devices)])  26.7 us
    ppermute x15, starting transfers between devices, swapped(): lax.ppermute(block, 'blk', [(i, i ^ distance) for i in range(devices)])  18.8 us
    pallas_call x1, Pallas kernels, weights_call(): pl.pallas_call(functools.partial(weights_kernel, n_q, n_kv), out_shape=[j...  1.42 us
    pallas_call x1, Pallas kernels, stage_call(): pl.pallas_call(stage_kernel, out_shape=[jax.ShapeDtypeStruct(a.shape, a.d...  1.06 us
  transfers between devices with their start and end apart: 15, of which 10 were waited for; matrix products, arithmetic and copies ran while one was open for 0% of the time, Pallas kernels for 8%

commit v1 on v0

--- a/solution.py
+++ b/solution.py
@@ -35,9 +35,17 @@
     return pltpu.with_memory_space_constraint(array, pltpu.MemorySpace.HBM)
 
 
-def limits_kernel(q_ref, last_ref, q_out, last, sems):
-    rows = q_ref.shape[0]
-    moves = ((last_ref, last), (q_ref, q_out.at[:, :WIDTH]))
+def stage_kernel(
+    q_ref, k_ref, v_ref, page_ref, last_ref, q_out, k_out, v_out, page, last, sems
+):
+    rows, tokens = q_ref.shape[0], k_ref.shape[0]
+    moves = (
+        (last_ref, last),
+        (q_ref, q_out.at[:, :WIDTH]),
+        (page_ref, page),
+        (k_ref, k_out.at[:tokens, :]),
+        (v_ref, v_out),
+    )
     copies = [pltpu.make_async_copy(s, d, sems.at[i]) for i, (s, d) in enumerate(moves)]
     for copy in copies:
         copy.start()
@@ -48,62 +56,51 @@
         jnp.logical_or, [(row == r) & (lane == last[r]) for r in range(rows)]
     )
     q_out[:, WIDTH:] = jnp.where(seen, 1.0, 0.0).astype(jnp.bfloat16)
-    copies[1].wait()
-
-
-def limits_call(queries, row_last):
-    rows = queries.shape[0]
-    return pl.pallas_call(
-        limits_kernel,
-        out_shape=jax.ShapeDtypeStruct((rows, WIDTH + LANES), jnp.bfloat16),
-        in_specs=[HBM_BLOCK] * 2,
-        out_specs=VMEM_BLOCK,
-        scratch_shapes=[pltpu.SMEM((rows,), jnp.int32), pltpu.SemaphoreType.DMA((2,))],
+    for copy in copies[1:]:
+        copy.wait()
+    filled = jnp.broadcast_to(page[...], (8, tokens)).astype(jnp.float32)
+    k_out[tokens:, :tokens] = filled.astype(jnp.bfloat16)
+    k_out[tokens:, tokens:] = jnp.zeros((8, k_out.shape[1] - tokens), jnp.bfloat16)
+
+
+def stage_call(row_last, queries, key_cache, value_cache, pages):
+    rows, (tokens, width) = queries.shape[0], key_cache.shape
+    return pl.pallas_call(
+        stage_kernel,
+        out_shape=[
+            jax.ShapeDtypeStruct((rows, WIDTH + LANES), jnp.bfloat16),
+            jax.ShapeDtypeStruct((tokens + 8, width), jnp.bfloat16),
+            jax.ShapeDtypeStruct(value_cache.shape, jnp.bfloat16),
+        ],
+        in_specs=[HBM_BLOCK] * 5,
+        out_specs=[VMEM_BLOCK] * 3,
+        scratch_shapes=[
+            pltpu.VMEM(pages.shape, jnp.int32),
+            pltpu.SMEM((rows,), jnp.int32),
+            pltpu.SemaphoreType.DMA((5,)),
+        ],
         compiler_params=pltpu.CompilerParams(vmem_limit_bytes=8 << 20),
-    )(in_hbm(queries), in_hbm(row_last))
-
-
-def stage_kernel(*refs):
-    sources, targets, sems = refs[: len(refs) // 2], refs[len(refs) // 2 : -1], refs[-1]
-    copies = [
-        pltpu.make_async_copy(source, target, sems.at[i])
-        for i, (source, target) in enumerate(zip(sources, targets))
-    ]
-    for copy in copies:
-        copy.start()
-    for copy in copies:
-        copy.wait()
-
-
-def stage_call(*arrays):
-    return pl.pallas_call(
-        stage_kernel,
-        out_shape=[jax.ShapeDtypeStruct(a.shape, a.dtype) for a in arrays],
-        in_specs=[HBM_BLOCK] * len(arrays),
-        out_specs=[VMEM_BLOCK] * len(arrays),
-        scratch_shapes=[pltpu.SemaphoreType.DMA((len(arrays),))],
-        compiler_params=pltpu.CompilerParams(vmem_limit_bytes=8 << 20),
-    )(*map(in_hbm, arrays))
+    )(*map(in_hbm, (queries, key_cache, value_cache, pages, row_last)))
 
 
 def weights_kernel(n_q, n_kv, *refs):
     q_refs, k_refs = refs[:n_q], refs[n_q : n_q + n_kv]
-    page_refs = refs[n_q + n_kv : n_q + 2 * n_kv]
-    weight_ref, top_ref = refs[n_q + 2 * n_kv :]
-    rows, tokens = q_refs[0].shape[0], k_refs[0].shape[0]
+    page_refs = refs[n_q + n_kv : n_q + n_kv + 2]
+    weight_ref, top_ref = refs[n_q + n_kv + 2 :]
+    rows, tokens = q_refs[0].shape[0], k_refs[-1].shape[0]
     lane = lax.broadcasted_iota(jnp.int32, (rows, LANES), 1)
     token_lane = lax.broadcasted_iota(jnp.int32, (tokens, LANES), 1).astype(jnp.float32)
     pick = jnp.where(
         lax.broadcasted_iota(jnp.int32, (8, LANES), 0) == 0, 1.0, 0.0
     ).astype(jnp.bfloat16)
     hides = []
+    page_rows = [ref[tokens:, :tokens] for ref in k_refs[:2]]
     for ref in page_refs:
         pages = jnp.broadcast_to(ref[...], (8, tokens)).astype(jnp.float32)
+        page_rows.append(pages.astype(jnp.bfloat16))
+    for pages in page_rows:
         column = lax.dot_general(
-            pages.astype(jnp.bfloat16),
-            pick,
-            (((0,), (0,)), ((), ())),
-            preferred_element_type=jnp.float32,
+            pages, pick, (((0,), (0,)), ((), ())), preferred_element_type=jnp.float32
         )
         hides.append(jnp.where(column > token_lane, FAR, 0.0).astype(jnp.bfloat16))
     tops = [jnp.zeros((rows, LANES), jnp.float32)] * n_q
@@ -119,7 +116,7 @@
         q_all = jnp.concatenate(parts, axis=0).astype(jnp.bfloat16)
         scores = []
         for ref, hide in zip(k_refs, hides):
-            k = ref[:, kv * HEAD_DIM : (kv + 1) * HEAD_DIM]
+            k = ref[:tokens, kv * HEAD_DIM : (kv + 1) * HEAD_DIM]
             scores.append(
                 lax.dot_general(
                     q_all,
@@ -191,14 +188,14 @@
 
 def weights_call(q_blocks, k_blocks, page_blocks):
     n_q, n_kv = len(q_blocks), len(k_blocks)
-    rows, tokens = q_blocks[0].shape[0], k_blocks[0].shape[0]
+    rows, tokens = q_blocks[0].shape[0], k_blocks[-1].shape[0]
     return pl.pallas_call(
         functools.partial(weights_kernel, n_q, n_kv),
         out_shape=[
             jax.ShapeDtypeStruct((n_q * HEADS * rows, n_kv * tokens), jnp.bfloat16),
             jax.ShapeDtypeStruct((n_q * rows, LANES), jnp.float32),
         ],
-        in_specs=[VMEM_BLOCK] * (n_q + 2 * n_kv),
+        in_specs=[VMEM_BLOCK] * (n_q + n_kv + 2),
         out_specs=[VMEM_BLOCK] * 2,
         compiler_params=pltpu.CompilerParams(vmem_limit_bytes=24 << 20),
     )(*q_blocks, *k_blocks, *page_blocks)
@@ -300,11 +297,13 @@
 def attend(queries, key_cache, value_cache, tile_page, row_last):
     groups = lax.axis_size("blk") // SHARE
     pages = tile_page.reshape(1, -1)
-    own_q = limits_call(queries, row_last)
-    own_k, own_v, own_page = stage_call(key_cache, value_cache, pages)
-    k_blocks = pooled(key_cache, own_k)
+    own_q, own_k, own_v = stage_call(row_last, queries, key_cache, value_cache, pages)
+    across = swapped(key_cache, 2)
+    k_blocks = [own_k, swapped(own_k, 1), across]
+    k_blocks.append(swapped(across, 1))
     v_blocks = pooled(value_cache, own_v)
-    page_blocks = pooled(pages, own_page)
+    across = swapped(pages, 2)
+    page_blocks = [across, swapped(across, 1)]
     q_blocks = [own_q] + [swapped(own_q, SHARE * d) for d in range(1, groups)]
     partials = []
     for start in range(0, groups, 4):

time: 51.1 us -> 49.7 us (0.973)
  Pallas kernels: 5.36 us -> 4.54 us
  waiting for transfers between devices: 26.7 us -> 25.9 us
    ppermute x15 -> x14, waiting for transfers between devices: 26.7 us -> 25.9 us  [swapped(): lax.ppermute(block, 'blk', [(i, i ^ distance) for i in range(devices)])]
    pallas_call x2 -> x1, Pallas kernels: 1.91 us -> 1.13 us  [stage_call(): pl.pallas_call(stage_kernel, out_shape=[jax.ShapeDtypeStruct((rows, WIDTH...]
    ppermute x15 -> x14, starting transfers between devices: 18.8 us -> 19 us  [swapped(): lax.ppermute(block, 'blk', [(i, i ^ distance) for i in range(devices)])]
  transfers between devices with their start and end apart: 15 -> 14, of which waited for: 10 -> 10; matrix products, arithmetic and copies ran while one was open for 0% -> 0% of each run, Pallas kernels for 8% -> 7%
where the time goes in v1:
time: 49.7 us; the launch traced here: 49.6 us
  waiting for transfers between devices  25.9 us (52%)
  starting transfers between devices  19 us (38%)
  Pallas kernels  4.54 us (9%)
    ppermute x14, waiting for transfers between devices, swapped(): lax.ppermute(block, 'blk', [(i, i ^ distance) for i in range(devices)])  25.9 us
    ppermute x14, starting transfers between devices, swapped(): lax.ppermute(block, 'blk', [(i, i ^ distance) for i in range(devices)])  19 us
    pallas_call x1, Pallas kernels, weights_call(): pl.pallas_call(functools.partial(weights_kernel, n_q, n_kv), out_shape=[j...  1.39 us
    pallas_call x1, Pallas kernels, stage_call(): pl.pallas_call(stage_kernel, out_shape=[jax.ShapeDtypeStruct((rows, WIDTH...  1.13 us
  transfers between devices with their start and end apart: 14, of which 10 were waited for; matrix products, arithmetic and copies ran while one was open for 0% of the time, Pallas kernels for 7%

profile of v1, /device:TPU:0, one launch (start us, length us, event | category | flops | bytes accessed | tf_op | source)
XLA Modules:
  0.0 49.6 jit_solution(4631115250899531313)
XLA Ops:
  0.0 3.0 %collective-permute-start.4 = (bf16[256,512]{1,0:T(8,128)(2,1)}, bf16[256,512]{1,0:T(8,128)(2,1)S(1)}, u32[]{:S(2)}, u32[]{:S(2)}) collective-permute-start(bf16[256,512]{1,0:T(8,128)(2,1)} %k_ref.1), channel_id=1, source_target_pairs={{0,2},{1,3},{2,0},{3,1},{4,6},{5,7},{6,4},{7,5},{8,10},{9,11},{10,... | collective-permute-start | bytes 786440 | tf_op jit(solution)/shard_map/ppermute | solution.py:25
  3.0 0.0 collective-permute-start.9
  3.0 1.1 %shard_map.55 = (bf16[8,4224]{1,0:T(8,128)(2,1)S(1)}, bf16[264,512]{1,0:T(8,128)(2,1)S(1)}, bf16[256,512]{1,0:T(8,128)(2,1)S(1)}) custom-call(bf16[8,4096]{1,0:T(8,128)(2,1)} %q_ref.1, bf16[256,512]{1,0:T(8,128)(2,1)} %k_ref.1, bf16[256,512]{1,0:T(8,128)(2,1)} %v_ref.1, s32[1,256]{1,0:T(1,128)} %bitcast.1, s32[8]{0:T(128)} %last_ref.1), custom_call_target="tpu_custom_call" | custom-call | tf_op jit(solution)/shard_map/pallas_call | solution.py:68
  4.2 0.1 collective-permute-start.3
  4.2 6.1 %collective-permute-done.4.refs_6_ = bf16[256,512]{1,0:T(8,128)(2,1)S(1)} collective-permute-done((bf16[256,512]{1,0:T(8,128)(2,1)}, bf16[256,512]{1,0:T(8,128)(2,1)S(1)}, u32[]{:S(2)}, u32[]{:S(2)}) %collective-permute-start.4) | collective-permute-done | bytes 262176 | tf_op jit(solution)/shard_map/ppermute | solution.py:25
  10.4 0.0 collective-permute-start.5
  10.4 0.5 %collective-permute-start.8 = (bf16[256,512]{1,0:T(8,128)(2,1)}, bf16[256,512]{1,0:T(8,128)(2,1)S(1)}, u32[]{:S(2)}, u32[]{:S(2)}) collective-permute-start(bf16[256,512]{1,0:T(8,128)(2,1)} %v_ref.1), channel_id=1, source_target_pairs={{0,1},{1,0},{2,3},{3,2},{4,5},{5,4},{6,7},{7,6},{8,9},{9,8},{10,11... | collective-permute-start | bytes 786440 | tf_op jit(solution)/shard_map/ppermute | solution.py:25
  10.9 4.3 %collective-permute-done.9.refs_2_ = bf16[256,512]{1,0:T(8,128)(2,1)S(1)} collective-permute-done((bf16[256,512]{1,0:T(8,128)(2,1)}, bf16[256,512]{1,0:T(8,128)(2,1)S(1)}, u32[]{:S(2)}, u32[]{:S(2)}) %collective-permute-start.9) | collective-permute-done | bytes 262176 | tf_op jit(solution)/shard_map/ppermute | solution.py:25
  15.1 0.0 collective-permute-start.10
  15.1 1.7 %collective-permute-start.6 = (s32[1,256]{1,0:T(1,128)}, s32[1,256]{1,0:T(1,128)S(1)}, u32[]{:S(2)}, u32[]{:S(2)}) collective-permute-start(s32[1,256]{1,0:T(1,128)} %bitcast.2), channel_id=1, source_target_pairs={{0,2},{1,3},{2,0},{3,1},{4,6},{5,7},{6,4},{7,5},{8,10},{9,11},{10,... | collective-permute-start | bytes 3080 | tf_op jit(solution)/shard_map/ppermute | solution.py:25
  16.9 2.0 %collective-permute-done.6.refs_8_ = s32[1,256]{1,0:T(1,128)S(1)} collective-permute-done((s32[1,256]{1,0:T(1,128)}, s32[1,256]{1,0:T(1,128)S(1)}, u32[]{:S(2)}, u32[]{:S(2)}) %collective-permute-start.6) | collective-permute-done | bytes 1056 | tf_op jit(solution)/shard_map/ppermute | solution.py:25
  18.9 0.0 collective-permute-start.7
  18.9 1.2 %collective-permute-done.7.refs_9_ = s32[1,256]{1,0:T(1,128)S(1)} collective-permute-done((s32[1,256]{1,0:T(1,128)S(1)}, s32[1,256]{1,0:T(1,128)S(1)}, u32[]{:S(2)}, u32[]{:S(2)}) %collective-permute-start.7) | collective-permute-done | bytes 1056 | tf_op jit(solution)/shard_map/ppermute | solution.py:25
  20.1 1.8 %collective-permute-start = (bf16[8,4224]{1,0:T(8,128)(2,1)S(1)}, bf16[8,4224]{1,0:T(8,128)(2,1)S(1)}, u32[]{:S(2)}, u32[]{:S(2)}) collective-permute-start(bf16[8,4224]{1,0:T(8,128)(2,1)S(1)} %get-tuple-element.16.refs_0_), channel_id=1, source_target_pairs={{0,4},{1,5},{2,6},{3,7},{4,0},{5,1},{6,2},{7,3},{8,12},{9,13},{10,... | collective-permute-start | bytes 202760 | tf_op jit(solution)/shard_map/ppermute | solution.py:25
  21.9 2.5 %collective-permute-done.refs_1_ = bf16[8,4224]{1,0:T(8,128)(2,1)S(1)} collective-permute-done((bf16[8,4224]{1,0:T(8,128)(2,1)S(1)}, bf16[8,4224]{1,0:T(8,128)(2,1)S(1)}, u32[]{:S(2)}, u32[]{:S(2)}) %collective-permute-start) | collective-permute-done | bytes 67616 | tf_op jit(solution)/shard_map/ppermute | solution.py:25
  24.4 2.8 %collective-permute-start.1 = (bf16[8,4224]{1,0:T(8,128)(2,1)S(1)}, bf16[8,4224]{1,0:T(8,128)(2,1)S(1)}, u32[]{:S(2)}, u32[]{:S(2)}) collective-permute-start(bf16[8,4224]{1,0:T(8,128)(2,1)S(1)} %get-tuple-element.16.refs_0_), channel_id=1, source_target_pairs={{0,8},{1,9},{2,10},{3,11},{4,12},{5,13},{6,14},{7,15},{8,0},{9,1},... | collective-permute-start | bytes 202760 | tf_op jit(solution)/shard_map/ppermute | solution.py:25
  27.2 2.4 %collective-permute-done.1.refs_2_ = bf16[8,4224]{1,0:T(8,128)(2,1)S(1)} collective-permute-done((bf16[8,4224]{1,0:T(8,128)(2,1)S(1)}, bf16[8,4224]{1,0:T(8,128)(2,1)S(1)}, u32[]{:S(2)}, u32[]{:S(2)}) %collective-permute-start.1) | collective-permute-done | bytes 67616 | tf_op jit(solution)/shard_map/ppermute | solution.py:25
  29.6 4.6 %collective-permute-start.2 = (bf16[8,4224]{1,0:T(8,128)(2,1)S(1)}, bf16[8,4224]{1,0:T(8,128)(2,1)S(1)}, u32[]{:S(2)}, u32[]{:S(2)}) collective-permute-start(bf16[8,4224]{1,0:T(8,128)(2,1)S(1)} %get-tuple-element.16.refs_0_), channel_id=1, source_target_pairs={{0,12},{1,13},{2,14},{3,15},{4,8},{5,9},{6,10},{7,11},{8,4},{9,5},... | collective-permute-start | bytes 202760 | tf_op jit(solution)/shard_map/ppermute | solution.py:25
  34.2 2.3 %collective-permute-done.2.refs_3_ = bf16[8,4224]{1,0:T(8,128)(2,1)S(1)} collective-permute-done((bf16[8,4224]{1,0:T(8,128)(2,1)S(1)}, bf16[8,4224]{1,0:T(8,128)(2,1)S(1)}, u32[]{:S(2)}, u32[]{:S(2)}) %collective-permute-start.2) | collective-permute-done | bytes 67616 | tf_op jit(solution)/shard_map/ppermute | solution.py:25
  36.4 0.0 collective-permute-done.3.refs_5_
  36.5 0.0 collective-permute-done.5.refs_7_
  36.5 1.4 %shard_map.56 = (bf16[1024,1024]{1,0:T(8,128)(2,1)S(1)}, f32[32,128]{1,0:T(8,128)S(1)}) custom-call(bf16[8,4224]{1,0:T(8,128)(2,1)S(1)} %get-tuple-element.16.refs_0_, bf16[8,4224]{1,0:T(8,128)(2,1)S(1)} %collective-permute-done.refs_1_, bf16[8,4224]{1,0:T(8,128)(2,1)S(1)} %collective-permute-done.1.refs_2_, ...), custom_call_target="tpu_custom_call" | custom-call | tf_op jit(solution)/shard_map/pallas_call | solution.py:192
  37.9 0.0 collective-permute-done.8.refs_1_
  37.9 0.6 %shard_map.57.sum_ref = f32[1024,256]{1,0:T(8,128)S(1)} custom-call(bf16[1024,1024]{1,0:T(8,128)(2,1)S(1)} %get-tuple-element.18.weight_ref, bf16[256,512]{1,0:T(8,128)(2,1)S(1)} %get-tuple-element.20.refs_0_, bf16[256,512]{1,0:T(8,128)(2,1)S(1)} %collective-permute-done.8.refs_1_, bf16[256,512]{1,0:T(8,128)(2,1)S(1)} %collective-permute-done.9.refs_2_), custom_call_target="tpu_custom_call" | custom-call | tf_op jit(solution)/shard_map/pallas_call | solution.py:205
  38.4 0.0 collective-permute-done.10.v_ref
  38.5 0.3 shard_map.58
  38.8 0.1 collective-permute-start.11
  38.9 3.9 %collective-permute-start.12 = (bf16[8,4224]{1,0:T(8,128)(2,1)S(1)}, bf16[8,4224]{1,0:T(8,128)(2,1)S(1)}, u32[]{:S(2)}, u32[]{:S(2)}) collective-permute-start(bf16[8,4224]{1,0:T(8,128)(2,1)S(1)} %get-tuple-element.23), channel_id=1, source_target_pairs={{0,12},{1,13},{2,14},{3,15},{4,8},{5,9},{6,10},{7,11},{8,4},{9,5},... | collective-permute-start | bytes 202760 | tf_op jit(solution)/shard_map/ppermute | solution.py:25
  42.8 0.5 collective-permute-start.13
  43.2 0.2 collective-permute-done.11.refs_1_
  43.4 2.3 %collective-permute-done.12.refs_2_ = bf16[8,4224]{1,0:T(8,128)(2,1)S(1)} collective-permute-done((bf16[8,4224]{1,0:T(8,128)(2,1)S(1)}, bf16[8,4224]{1,0:T(8,128)(2,1)S(1)}, u32[]{:S(2)}, u32[]{:S(2)}) %collective-permute-start.12) | collective-permute-done | bytes 67616 | tf_op jit(solution)/shard_map/ppermute | solution.py:25
  45.8 0.2 shard_map.59
  46.0 2.7 %collective-permute-done.13.part_ref = bf16[8,4224]{1,0:T(8,128)(2,1)S(1)} collective-permute-done((bf16[8,4224]{1,0:T(8,128)(2,1)S(1)}, bf16[8,4224]{1,0:T(8,128)(2,1)S(1)}, u32[]{:S(2)}, u32[]{:S(2)}) %collective-permute-start.13) | collective-permute-done | bytes 67616 | tf_op jit(solution)/shard_map/ppermute | solution.py:25
  48.7 0.9 %shard_map.60 = bf16[8,4096]{1,0:T(8,128)(2,1)} custom-call(f32[8,4096]{1,0:T(8,128)S(1)} %get-tuple-element.24.sum_ref, f32[8,256]{1,0:T(8,128)S(1)} %get-tuple-element.25.stat_ref, bf16[8,4224]{1,0:T(8,128)(2,1)S(1)} %collective-permute-done.13.part_ref), custom_call_target="tpu_custom_call" | custom-call | tf_op jit(solution)/shard_map/pallas_call | solution.py:282
Async XLA Ops:
  0.0 10.4 %collective-permute-start.4 = (bf16[256,512]{1,0:T(8,128)(2,1)}, bf16[256,512]{1,0:T(8,128)(2,1)S(1)}, u32[]{:S(2)}, u32[]{:S(2)}) collective-permute-start(bf16[256,512]{1,0:T(8,128)(2,1)} %k_ref.1), channel_id=1, source_target_pairs={{0,2},{1,3},{2,0},{3,1},{4,6},{5,7},{6,4},{7,5},{8,10},{9,11},{10,... | collective-permute-start | bytes 786440 | tf_op jit(solution)/shard_map/ppermute | solution.py:25
  3.0 12.1 %collective-permute-start.9 = (bf16[256,512]{1,0:T(8,128)(2,1)}, bf16[256,512]{1,0:T(8,128)(2,1)S(1)}, u32[]{:S(2)}, u32[]{:S(2)}) collective-permute-start(bf16[256,512]{1,0:T(8,128)(2,1)} %v_ref.1), channel_id=1, source_target_pairs={{0,2},{1,3},{2,0},{3,1},{4,6},{5,7},{6,4},{7,5},{8,10},{9,11},{10,... | collective-permute-start | bytes 786440 | tf_op jit(solution)/shard_map/ppermute | solution.py:25
  4.2 32.3 %collective-permute-start.3 = (bf16[264,512]{1,0:T(8,128)(2,1)S(1)}, bf16[264,512]{1,0:T(8,128)(2,1)S(1)}, u32[]{:S(2)}, u32[]{:S(2)}) collective-permute-start(bf16[264,512]{1,0:T(8,128)(2,1)S(1)} %get-tuple-element.17.refs_4_), channel_id=1, source_target_pairs={{0,1},{1,0},{2,3},{3,2},{4,5},{5,4},{6,7},{7,6},{8,9},{9,8},{10,11... | collective-permute-start | bytes 811016 | tf_op jit(solution)/shard_map/ppermute | solution.py:25
  10.4 26.1 %collective-permute-start.5 = (bf16[256,512]{1,0:T(8,128)(2,1)S(1)}, bf16[256,512]{1,0:T(8,128)(2,1)S(1)}, u32[]{:S(2)}, u32[]{:S(2)}) collective-permute-start(bf16[256,512]{1,0:T(8,128)(2,1)S(1)} %collective-permute-done.4.refs_6_), channel_id=1, source_target_pairs={{0,1},{1,0},{2,3},{3,2},{4,5},{5,4},{6,7},{7,6},{8,9},{9,8},{10,11... | collective-permute-start | bytes 786440 | tf_op jit(solution)/shard_map/ppermute | solution.py:25
  10.4 27.5 %collective-permute-start.8 = (bf16[256,512]{1,0:T(8,128)(2,1)}, bf16[256,512]{1,0:T(8,128)(2,1)S(1)}, u32[]{:S(2)}, u32[]{:S(2)}) collective-permute-start(bf16[256,512]{1,0:T(8,128)(2,1)} %v_ref.1), channel_id=1, source_target_pairs={{0,1},{1,0},{2,3},{3,2},{4,5},{5,4},{6,7},{7,6},{8,9},{9,8},{10,11... | collective-permute-start | bytes 786440 | tf_op jit(solution)/shard_map/ppermute | solution.py:25
  15.1 23.3 %collective-permute-start.10 = (bf16[256,512]{1,0:T(8,128)(2,1)S(1)}, bf16[256,512]{1,0:T(8,128)(2,1)S(1)}, u32[]{:S(2)}, u32[]{:S(2)}) collective-permute-start(bf16[256,512]{1,0:T(8,128)(2,1)S(1)} %collective-permute-done.9.refs_2_), channel_id=1, source_target_pairs={{0,1},{1,0},{2,3},{3,2},{4,5},{5,4},{6,7},{7,6},{8,9},{9,8},{10,11... | collective-permute-start | bytes 786440 | tf_op jit(solution)/shard_map/ppermute | solution.py:25
  15.1 3.8 %collective-permute-start.6 = (s32[1,256]{1,0:T(1,128)}, s32[1,256]{1,0:T(1,128)S(1)}, u32[]{:S(2)}, u32[]{:S(2)}) collective-permute-start(s32[1,256]{1,0:T(1,128)} %bitcast.2), channel_id=1, source_target_pairs={{0,2},{1,3},{2,0},{3,1},{4,6},{5,7},{6,4},{7,5},{8,10},{9,11},{10,... | collective-permute-start | bytes 3080 | tf_op jit(solution)/shard_map/ppermute | solution.py:25
  18.9 1.2 %collective-permute-start.7 = (s32[1,256]{1,0:T(1,128)S(1)}, s32[1,256]{1,0:T(1,128)S(1)}, u32[]{:S(2)}, u32[]{:S(2)}) collective-permute-start(s32[1,256]{1,0:T(1,128)S(1)} %collective-permute-done.6.refs_8_), channel_id=1, source_target_pairs={{0,1},{1,0},{2,3},{3,2},{4,5},{5,4},{6,7},{7,6},{8,9},{9,8},{10,11... | collective-permute-start | bytes 3080 | tf_op jit(solution)/shard_map/ppermute | solution.py:25
  20.1 4.3 %collective-permute-start = (bf16[8,4224]{1,0:T(8,128)(2,1)S(1)}, bf16[8,4224]{1,0:T(8,128)(2,1)S(1)}, u32[]{:S(2)}, u32[]{:S(2)}) collective-permute-start(bf16[8,4224]{1,0:T(8,128)(2,1)S(1)} %get-tuple-element.16.refs_0_), channel_id=1, source_target_pairs={{0,4},{1,5},{2,6},{3,7},{4,0},{5,1},{6,2},{7,3},{8,12},{9,13},{10,... | collective-permute-start | bytes 202760 | tf_op jit(solution)/shard_map/ppermute | solution.py:25
  24.4 5.2 %collective-permute-start.1 = (bf16[8,4224]{1,0:T(8,128)(2,1)S(1)}, bf16[8,4224]{1,0:T(8,128)(2,1)S(1)}, u32[]{:S(2)}, u32[]{:S(2)}) collective-permute-start(bf16[8,4224]{1,0:T(8,128)(2,1)S(1)} %get-tuple-element.16.refs_0_), channel_id=1, source_target_pairs={{0,8},{1,9},{2,10},{3,11},{4,12},{5,13},{6,14},{7,15},{8,0},{9,1},... | collective-permute-start | bytes 202760 | tf_op jit(solution)/shard_map/ppermute | solution.py:25
  29.6 6.9 %collective-permute-start.2 = (bf16[8,4224]{1,0:T(8,128)(2,1)S(1)}, bf16[8,4224]{1,0:T(8,128)(2,1)S(1)}, u32[]{:S(2)}, u32[]{:S(2)}) collective-permute-start(bf16[8,4224]{1,0:T(8,128)(2,1)S(1)} %get-tuple-element.16.refs_0_), channel_id=1, source_target_pairs={{0,12},{1,13},{2,14},{3,15},{4,8},{5,9},{6,10},{7,11},{8,4},{9,5},... | collective-permute-start | bytes 202760 | tf_op jit(solution)/shard_map/ppermute | solution.py:25
  38.8 4.7 %collective-permute-start.11 = (bf16[8,4224]{1,0:T(8,128)(2,1)S(1)}, bf16[8,4224]{1,0:T(8,128)(2,1)S(1)}, u32[]{:S(2)}, u32[]{:S(2)}) collective-permute-start(bf16[8,4224]{1,0:T(8,128)(2,1)S(1)} %get-tuple-element.22), channel_id=1, source_target_pairs={{0,4},{1,5},{2,6},{3,7},{4,0},{5,1},{6,2},{7,3},{8,12},{9,13},{10,... | collective-permute-start | bytes 202760 | tf_op jit(solution)/shard_map/ppermute | solution.py:25
  38.9 6.9 %collective-permute-start.12 = (bf16[8,4224]{1,0:T(8,128)(2,1)S(1)}, bf16[8,4224]{1,0:T(8,128)(2,1)S(1)}, u32[]{:S(2)}, u32[]{:S(2)}) collective-permute-start(bf16[8,4224]{1,0:T(8,128)(2,1)S(1)} %get-tuple-element.23), channel_id=1, source_target_pairs={{0,12},{1,13},{2,14},{3,15},{4,8},{5,9},{6,10},{7,11},{8,4},{9,5},... | collective-permute-start | bytes 202760 | tf_op jit(solution)/shard_map/ppermute | solution.py:25
  42.8 5.9 %collective-permute-start.13 = (bf16[8,4224]{1,0:T(8,128)(2,1)S(1)}, bf16[8,4224]{1,0:T(8,128)(2,1)S(1)}, u32[]{:S(2)}, u32[]{:S(2)}) collective-permute-start(bf16[8,4224]{1,0:T(8,128)(2,1)S(1)} %get-tuple-element.26), channel_id=1, source_target_pairs={{0,8},{1,9},{2,10},{3,11},{4,12},{5,13},{6,14},{7,15},{8,0},{9,1},... | collective-permute-start | bytes 202760 | tf_op jit(solution)/shard_map/ppermute | solution.py:25

commit v2 on v1

--- a/solution.py
+++ b/solution.py
@@ -36,14 +36,14 @@
 
 
 def stage_kernel(
-    q_ref, k_ref, v_ref, page_ref, last_ref, q_out, k_out, v_out, page, last, sems
+    q_ref, k_ref, v_ref, page_ref, last_ref, q_out, k_out, v_out, page_out, last, sems
 ):
-    rows, tokens = q_ref.shape[0], k_ref.shape[0]
+    rows = q_ref.shape[0]
     moves = (
         (last_ref, last),
         (q_ref, q_out.at[:, :WIDTH]),
-        (page_ref, page),
-        (k_ref, k_out.at[:tokens, :]),
+        (page_ref, page_out),
+        (k_ref, k_out),
         (v_ref, v_out),
     )
     copies = [pltpu.make_async_copy(s, d, sems.at[i]) for i, (s, d) in enumerate(moves)]
@@ -58,49 +58,43 @@
     q_out[:, WIDTH:] = jnp.where(seen, 1.0, 0.0).astype(jnp.bfloat16)
     for copy in copies[1:]:
         copy.wait()
-    filled = jnp.broadcast_to(page[...], (8, tokens)).astype(jnp.float32)
-    k_out[tokens:, :tokens] = filled.astype(jnp.bfloat16)
-    k_out[tokens:, tokens:] = jnp.zeros((8, k_out.shape[1] - tokens), jnp.bfloat16)
 
 
 def stage_call(row_last, queries, key_cache, value_cache, pages):
-    rows, (tokens, width) = queries.shape[0], key_cache.shape
+    rows = queries.shape[0]
     return pl.pallas_call(
         stage_kernel,
         out_shape=[
             jax.ShapeDtypeStruct((rows, WIDTH + LANES), jnp.bfloat16),
-            jax.ShapeDtypeStruct((tokens + 8, width), jnp.bfloat16),
+            jax.ShapeDtypeStruct(key_cache.shape, jnp.bfloat16),
             jax.ShapeDtypeStruct(value_cache.shape, jnp.bfloat16),
+            jax.ShapeDtypeStruct(pages.shape, jnp.int32),
         ],
         in_specs=[HBM_BLOCK] * 5,
-        out_specs=[VMEM_BLOCK] * 3,
-        scratch_shapes=[
-            pltpu.VMEM(pages.shape, jnp.int32),
-            pltpu.SMEM((rows,), jnp.int32),
-            pltpu.SemaphoreType.DMA((5,)),
-        ],
+        out_specs=[VMEM_BLOCK] * 4,
+        scratch_shapes=[pltpu.SMEM((rows,), jnp.int32), pltpu.SemaphoreType.DMA((5,))],
         compiler_params=pltpu.CompilerParams(vmem_limit_bytes=8 << 20),
     )(*map(in_hbm, (queries, key_cache, value_cache, pages, row_last)))
 
 
 def weights_kernel(n_q, n_kv, *refs):
     q_refs, k_refs = refs[:n_q], refs[n_q : n_q + n_kv]
-    page_refs = refs[n_q + n_kv : n_q + n_kv + 2]
-    weight_ref, top_ref = refs[n_q + n_kv + 2 :]
-    rows, tokens = q_refs[0].shape[0], k_refs[-1].shape[0]
+    page_refs = refs[n_q + n_kv : n_q + 2 * n_kv]
+    weight_ref, top_ref = refs[n_q + 2 * n_kv :]
+    rows, tokens = q_refs[0].shape[0], k_refs[0].shape[0]
     lane = lax.broadcasted_iota(jnp.int32, (rows, LANES), 1)
     token_lane = lax.broadcasted_iota(jnp.int32, (tokens, LANES), 1).astype(jnp.float32)
     pick = jnp.where(
         lax.broadcasted_iota(jnp.int32, (8, LANES), 0) == 0, 1.0, 0.0
     ).astype(jnp.bfloat16)
     hides = []
-    page_rows = [ref[tokens:, :tokens] for ref in k_refs[:2]]
     for ref in page_refs:
         pages = jnp.broadcast_to(ref[...], (8, tokens)).astype(jnp.float32)
-        page_rows.append(pages.astype(jnp.bfloat16))
-    for pages in page_rows:
         column = lax.dot_general(
-            pages, pick, (((0,), (0,)), ((), ())), preferred_element_type=jnp.float32
+            pages.astype(jnp.bfloat16),
+            pick,
+            (((0,), (0,)), ((), ())),
+            preferred_element_type=jnp.float32,
         )
         hides.append(jnp.where(column > token_lane, FAR, 0.0).astype(jnp.bfloat16))
     tops = [jnp.zeros((rows, LANES), jnp.float32)] * n_q
@@ -116,7 +110,7 @@
         q_all = jnp.concatenate(parts, axis=0).astype(jnp.bfloat16)
         scores = []
         for ref, hide in zip(k_refs, hides):
-            k = ref[:tokens, kv * HEAD_DIM : (kv + 1) * HEAD_DIM]
+            k = ref[:, kv * HEAD_DIM : (kv + 1) * HEAD_DIM]
             scores.append(
                 lax.dot_general(
                     q_all,
@@ -188,14 +182,14 @@
 
 def weights_call(q_blocks, k_blocks, page_blocks):
     n_q, n_kv = len(q_blocks), len(k_blocks)
-    rows, tokens = q_blocks[0].shape[0], k_blocks[-1].shape[0]
+    rows, tokens = q_blocks[0].shape[0], k_blocks[0].shape[0]
     return pl.pallas_call(
         functools.partial(weights_kernel, n_q, n_kv),
         out_shape=[
             jax.ShapeDtypeStruct((n_q * HEADS * rows, n_kv * tokens), jnp.bfloat16),
             jax.ShapeDtypeStruct((n_q * rows, LANES), jnp.float32),
         ],
-        in_specs=[VMEM_BLOCK] * (n_q + n_kv + 2),
+        in_specs=[VMEM_BLOCK] * (n_q + 2 * n_kv),
         out_specs=[VMEM_BLOCK] * 2,
         compiler_params=pltpu.CompilerParams(vmem_limit_bytes=24 << 20),
     )(*q_blocks, *k_blocks, *page_blocks)
@@ -297,13 +291,12 @@
 def attend(queries, key_cache, value_cache, tile_page, row_last):
     groups = lax.axis_size("blk") // SHARE
     pages = tile_page.reshape(1, -1)
-    own_q, own_k, own_v = stage_call(row_last, queries, key_cache, value_cache, pages)
-    across = swapped(key_cache, 2)
-    k_blocks = [own_k, swapped(own_k, 1), across]
-    k_blocks.append(swapped(across, 1))
+    own_q, own_k, own_v, own_page = stage_call(
+        row_last, queries, key_cache, value_cache, pages
+    )
+    k_blocks = pooled(key_cache, own_k)
     v_blocks = pooled(value_cache, own_v)
-    across = swapped(pages, 2)
-    page_blocks = [across, swapped(across, 1)]
+    page_blocks = pooled(pages, own_page)
     q_blocks = [own_q] + [swapped(own_q, SHARE * d) for d in range(1, groups)]
     partials = []
     for start in range(0, groups, 4):

time: 49.7 us -> 51.5 us (1.036)
  waiting for transfers between devices: 25.9 us -> 29.3 us
  starting transfers between devices: 19 us -> 17.4 us
    ppermute x14 -> x15, waiting for transfers between devices: 25.9 us -> 29.3 us  [swapped(): lax.ppermute(block, 'blk', [(i, i ^ distance) for i in range(devices)])]
    ppermute x14 -> x15, starting transfers between devices: 19 us -> 17.4 us  [swapped(): lax.ppermute(block, 'blk', [(i, i ^ distance) for i in range(devices)])]
  transfers between devices with their start and end apart: 14 -> 15, of which waited for: 10 -> 10; matrix products, arithmetic and copies ran while one was open for 0% -> 0% of each run, Pallas kernels for 7% -> 6%
where the time goes in v2:
time: 51.5 us; the launch traced here: 51.4 us
  waiting for transfers between devices  29.3 us (57%)
  starting transfers between devices  17.4 us (34%)
  Pallas kernels  4.55 us (9%)
    ppermute x15, waiting for transfers between devices, swapped(): lax.ppermute(block, 'blk', [(i, i ^ distance) for i in range(devices)])  29.3 us
    ppermute x15, starting transfers between devices, swapped(): lax.ppermute(block, 'blk', [(i, i ^ distance) for i in range(devices)])  17.4 us
    pallas_call x1, Pallas kernels, weights_call(): pl.pallas_call(functools.partial(weights_kernel, n_q, n_kv), out_shape=[j...  1.41 us
    pallas_call x1, Pallas kernels, stage_call(): pl.pallas_call(stage_kernel, out_shape=[jax.ShapeDtypeStruct((rows, WIDTH...  1.13 us
  transfers between devices with their start and end apart: 15, of which 10 were waited for; matrix products, arithmetic and copies ran while one was open for 0% of the time, Pallas kernels for 6%

profile of v2, /device:TPU:0, one launch (start us, length us, event | category | flops | bytes accessed | tf_op | source)
XLA Modules:
  0.0 51.4 jit_solution(3023429659689992164)
XLA Ops:
  0.0 3.0 %collective-permute-start.4 = (bf16[256,512]{1,0:T(8,128)(2,1)}, bf16[256,512]{1,0:T(8,128)(2,1)S(1)}, u32[]{:S(2)}, u32[]{:S(2)}) collective-permute-start(bf16[256,512]{1,0:T(8,128)(2,1)} %k_ref.1), channel_id=1, source_target_pairs={{0,2},{1,3},{2,0},{3,1},{4,6},{5,7},{6,4},{7,5},{8,10},{9,11},{10,... | collective-permute-start | bytes 786440 | tf_op jit(solution)/shard_map/ppermute | solution.py:25
  3.0 0.0 collective-permute-start.10
  3.0 0.0 collective-permute-start.3
  3.0 7.3 %collective-permute-done.4.refs_6_ = bf16[256,512]{1,0:T(8,128)(2,1)S(1)} collective-permute-done((bf16[256,512]{1,0:T(8,128)(2,1)}, bf16[256,512]{1,0:T(8,128)(2,1)S(1)}, u32[]{:S(2)}, u32[]{:S(2)}) %collective-permute-start.4) | collective-permute-done | bytes 262176 | tf_op jit(solution)/shard_map/ppermute | solution.py:25
  10.4 0.0 collective-permute-start.5
  10.4 0.5 collective-permute-start.9
  10.9 4.3 %collective-permute-done.10.refs_2_ = bf16[256,512]{1,0:T(8,128)(2,1)S(1)} collective-permute-done((bf16[256,512]{1,0:T(8,128)(2,1)}, bf16[256,512]{1,0:T(8,128)(2,1)S(1)}, u32[]{:S(2)}, u32[]{:S(2)}) %collective-permute-start.10) | collective-permute-done | bytes 262176 | tf_op jit(solution)/shard_map/ppermute | solution.py:25
  15.1 0.0 collective-permute-start.11
  15.1 0.5 collective-permute-start.6
  15.6 1.0 %collective-permute-done.6.refs_9_ = s32[1,256]{1,0:T(1,128)S(1)} collective-permute-done((s32[1,256]{1,0:T(1,128)}, s32[1,256]{1,0:T(1,128)S(1)}, u32[]{:S(2)}, u32[]{:S(2)}) %collective-permute-start.6) | collective-permute-done | bytes 1056 | tf_op jit(solution)/shard_map/ppermute | solution.py:25
  16.7 1.7 %collective-permute-start.7 = (s32[1,256]{1,0:T(1,128)}, s32[1,256]{1,0:T(1,128)S(1)}, u32[]{:S(2)}, u32[]{:S(2)}) collective-permute-start(s32[1,256]{1,0:T(1,128)} %bitcast.2), channel_id=1, source_target_pairs={{0,2},{1,3},{2,0},{3,1},{4,6},{5,7},{6,4},{7,5},{8,10},{9,11},{10,... | collective-permute-start | bytes 3080 | tf_op jit(solution)/shard_map/ppermute | solution.py:25
  18.4 2.0 %collective-permute-done.7.refs_10_ = s32[1,256]{1,0:T(1,128)S(1)} collective-permute-done((s32[1,256]{1,0:T(1,128)}, s32[1,256]{1,0:T(1,128)S(1)}, u32[]{:S(2)}, u32[]{:S(2)}) %collective-permute-start.7) | collective-permute-done | bytes 1056 | tf_op jit(solution)/shard_map/ppermute | solution.py:25
  20.5 0.0 collective-permute-start.8
  20.5 1.1 %shard_map.55 = (bf16[8,4224]{1,0:T(8,128)(2,1)S(1)}, bf16[256,512]{1,0:T(8,128)(2,1)S(1)}, bf16[256,512]{1,0:T(8,128)(2,1)S(1)}, s32[1,256]{1,0:T(1,128)S(1)}) custom-call(bf16[8,4096]{1,0:T(8,128)(2,1)} %q_ref.1, bf16[256,512]{1,0:T(8,128)(2,1)} %k_ref.1, bf16[256,512]{1,0:T(8,128)(2,1)} %v_ref.1, s32[1,256]{1,0:T(1,128)} %bitcast.3, s32[8]{0:T(128)} %last_ref.1), custom_call_target="tpu_custom_call" | custom-call | tf_op jit(solution)/shard_map/pallas_call | solution.py:65
  21.6 0.0 collective-permute-done.8.refs_11_
  21.6 1.9 %collective-permute-start = (bf16[8,4224]{1,0:T(8,128)(2,1)S(1)}, bf16[8,4224]{1,0:T(8,128)(2,1)S(1)}, u32[]{:S(2)}, u32[]{:S(2)}) collective-permute-start(bf16[8,4224]{1,0:T(8,128)(2,1)S(1)} %get-tuple-element.17.refs_0_), channel_id=1, source_target_pairs={{0,4},{1,5},{2,6},{3,7},{4,0},{5,1},{6,2},{7,3},{8,12},{9,13},{10,... | collective-permute-start | bytes 202760 | tf_op jit(solution)/shard_map/ppermute | solution.py:25
  23.5 2.8 %collective-permute-done.refs_1_ = bf16[8,4224]{1,0:T(8,128)(2,1)S(1)} collective-permute-done((bf16[8,4224]{1,0:T(8,128)(2,1)S(1)}, bf16[8,4224]{1,0:T(8,128)(2,1)S(1)}, u32[]{:S(2)}, u32[]{:S(2)}) %collective-permute-start) | collective-permute-done | bytes 67616 | tf_op jit(solution)/shard_map/ppermute | solution.py:25
  26.3 2.8 %collective-permute-start.1 = (bf16[8,4224]{1,0:T(8,128)(2,1)S(1)}, bf16[8,4224]{1,0:T(8,128)(2,1)S(1)}, u32[]{:S(2)}, u32[]{:S(2)}) collective-permute-start(bf16[8,4224]{1,0:T(8,128)(2,1)S(1)} %get-tuple-element.17.refs_0_), channel_id=1, source_target_pairs={{0,8},{1,9},{2,10},{3,11},{4,12},{5,13},{6,14},{7,15},{8,0},{9,1},... | collective-permute-start | bytes 202760 | tf_op jit(solution)/shard_map/ppermute | solution.py:25
  29.0 3.7 %collective-permute-done.1.refs_2_ = bf16[8,4224]{1,0:T(8,128)(2,1)S(1)} collective-permute-done((bf16[8,4224]{1,0:T(8,128)(2,1)S(1)}, bf16[8,4224]{1,0:T(8,128)(2,1)S(1)}, u32[]{:S(2)}, u32[]{:S(2)}) %collective-permute-start.1) | collective-permute-done | bytes 67616 | tf_op jit(solution)/shard_map/ppermute | solution.py:25
  32.8 3.2 %collective-permute-start.2 = (bf16[8,4224]{1,0:T(8,128)(2,1)S(1)}, bf16[8,4224]{1,0:T(8,128)(2,1)S(1)}, u32[]{:S(2)}, u32[]{:S(2)}) collective-permute-start(bf16[8,4224]{1,0:T(8,128)(2,1)S(1)} %get-tuple-element.17.refs_0_), channel_id=1, source_target_pairs={{0,12},{1,13},{2,14},{3,15},{4,8},{5,9},{6,10},{7,11},{8,4},{9,5},... | collective-permute-start | bytes 202760 | tf_op jit(solution)/shard_map/ppermute | solution.py:25
  36.0 2.9 %collective-permute-done.2.refs_3_ = bf16[8,4224]{1,0:T(8,128)(2,1)S(1)} collective-permute-done((bf16[8,4224]{1,0:T(8,128)(2,1)S(1)}, bf16[8,4224]{1,0:T(8,128)(2,1)S(1)}, u32[]{:S(2)}, u32[]{:S(2)}) %collective-permute-start.2) | collective-permute-done | bytes 67616 | tf_op jit(solution)/shard_map/ppermute | solution.py:25
  38.9 0.0 collective-permute-done.3.refs_5_
  38.9 0.0 collective-permute-done.5.refs_7_
  38.9 1.4 %shard_map.56 = (bf16[1024,1024]{1,0:T(8,128)(2,1)S(1)}, f32[32,128]{1,0:T(8,128)S(1)}) custom-call(bf16[8,4224]{1,0:T(8,128)(2,1)S(1)} %get-tuple-element.17.refs_0_, bf16[8,4224]{1,0:T(8,128)(2,1)S(1)} %collective-permute-done.refs_1_, bf16[8,4224]{1,0:T(8,128)(2,1)S(1)} %collective-permute-done.1.refs_2_, ...), custom_call_target="tpu_custom_call" | custom-call | tf_op jit(solution)/shard_map/pallas_call | solution.py:186
  40.3 0.0 collective-permute-done.9.refs_1_
  40.3 0.6 %shard_map.57.sum_ref = f32[1024,256]{1,0:T(8,128)S(1)} custom-call(bf16[1024,1024]{1,0:T(8,128)(2,1)S(1)} %get-tuple-element.20.weight_ref, bf16[256,512]{1,0:T(8,128)(2,1)S(1)} %get-tuple-element.22.refs_0_, bf16[256,512]{1,0:T(8,128)(2,1)S(1)} %collective-permute-done.9.refs_1_, bf16[256,512]{1,0:T(8,128)(2,1)S(1)} %collective-permute-done.10.refs_2_), custom_call_target="tpu_custom_call" | custom-call | tf_op jit(solution)/shard_map/pallas_call | solution.py:199
  40.9 0.0 collective-permute-done.11.v_ref
  40.9 0.3 shard_map.58
  41.2 0.1 collective-permute-start.12
  41.3 3.3 %collective-permute-start.13 = (bf16[8,4224]{1,0:T(8,128)(2,1)S(1)}, bf16[8,4224]{1,0:T(8,128)(2,1)S(1)}, u32[]{:S(2)}, u32[]{:S(2)}) collective-permute-start(bf16[8,4224]{1,0:T(8,128)(2,1)S(1)} %get-tuple-element.25), channel_id=1, source_target_pairs={{0,12},{1,13},{2,14},{3,15},{4,8},{5,9},{6,10},{7,11},{8,4},{9,5},... | collective-permute-start | bytes 202760 | tf_op jit(solution)/shard_map/ppermute | solution.py:25
  44.6 0.5 collective-permute-start.14
  45.1 0.8 %collective-permute-done.12.refs_1_ = bf16[8,4224]{1,0:T(8,128)(2,1)S(1)} collective-permute-done((bf16[8,4224]{1,0:T(8,128)(2,1)S(1)}, bf16[8,4224]{1,0:T(8,128)(2,1)S(1)}, u32[]{:S(2)}, u32[]{:S(2)}) %collective-permute-start.12) | collective-permute-done | bytes 67616 | tf_op jit(solution)/shard_map/ppermute | solution.py:25
  45.9 2.4 %collective-permute-done.13.refs_2_ = bf16[8,4224]{1,0:T(8,128)(2,1)S(1)} collective-permute-done((bf16[8,4224]{1,0:T(8,128)(2,1)S(1)}, bf16[8,4224]{1,0:T(8,128)(2,1)S(1)}, u32[]{:S(2)}, u32[]{:S(2)}) %collective-permute-start.13) | collective-permute-done | bytes 67616 | tf_op jit(solution)/shard_map/ppermute | solution.py:25
  48.3 0.2 shard_map.59
  48.5 1.9 %collective-permute-done.14.part_ref = bf16[8,4224]{1,0:T(8,128)(2,1)S(1)} collective-permute-done((bf16[8,4224]{1,0:T(8,128)(2,1)S(1)}, bf16[8,4224]{1,0:T(8,128)(2,1)S(1)}, u32[]{:S(2)}, u32[]{:S(2)}) %collective-permute-start.14) | collective-permute-done | bytes 67616 | tf_op jit(solution)/shard_map/ppermute | solution.py:25
  50.5 0.9 %shard_map.60 = bf16[8,4096]{1,0:T(8,128)(2,1)} custom-call(f32[8,4096]{1,0:T(8,128)S(1)} %get-tuple-element.26.sum_ref, f32[8,256]{1,0:T(8,128)S(1)} %get-tuple-element.27.stat_ref, bf16[8,4224]{1,0:T(8,128)(2,1)S(1)} %collective-permute-done.14.part_ref), custom_call_target="tpu_custom_call" | custom-call | tf_op jit(solution)/shard_map/pallas_call | solution.py:276
Async XLA Ops:
  0.0 10.4 %collective-permute-start.4 = (bf16[256,512]{1,0:T(8,128)(2,1)}, bf16[256,512]{1,0:T(8,128)(2,1)S(1)}, u32[]{:S(2)}, u32[]{:S(2)}) collective-permute-start(bf16[256,512]{1,0:T(8,128)(2,1)} %k_ref.1), channel_id=1, source_target_pairs={{0,2},{1,3},{2,0},{3,1},{4,6},{5,7},{6,4},{7,5},{8,10},{9,11},{10,... | collective-permute-start | bytes 786440 | tf_op jit(solution)/shard_map/ppermute | solution.py:25
  3.0 12.1 %collective-permute-start.10 = (bf16[256,512]{1,0:T(8,128)(2,1)}, bf16[256,512]{1,0:T(8,128)(2,1)S(1)}, u32[]{:S(2)}, u32[]{:S(2)}) collective-permute-start(bf16[256,512]{1,0:T(8,128)(2,1)} %v_ref.1), channel_id=1, source_target_pairs={{0,2},{1,3},{2,0},{3,1},{4,6},{5,7},{6,4},{7,5},{8,10},{9,11},{10,... | collective-permute-start | bytes 786440 | tf_op jit(solution)/shard_map/ppermute | solution.py:25
  3.0 35.8 %collective-permute-start.3 = (bf16[256,512]{1,0:T(8,128)(2,1)}, bf16[256,512]{1,0:T(8,128)(2,1)S(1)}, u32[]{:S(2)}, u32[]{:S(2)}) collective-permute-start(bf16[256,512]{1,0:T(8,128)(2,1)} %k_ref.1), channel_id=1, source_target_pairs={{0,1},{1,0},{2,3},{3,2},{4,5},{5,4},{6,7},{7,6},{8,9},{9,8},{10,11... | collective-permute-start | bytes 786440 | tf_op jit(solution)/shard_map/ppermute | solution.py:25
  10.4 28.5 %collective-permute-start.5 = (bf16[256,512]{1,0:T(8,128)(2,1)S(1)}, bf16[256,512]{1,0:T(8,128)(2,1)S(1)}, u32[]{:S(2)}, u32[]{:S(2)}) collective-permute-start(bf16[256,512]{1,0:T(8,128)(2,1)S(1)} %collective-permute-done.4.refs_6_), channel_id=1, source_target_pairs={{0,1},{1,0},{2,3},{3,2},{4,5},{5,4},{6,7},{7,6},{8,9},{9,8},{10,11... | collective-permute-start | bytes 786440 | tf_op jit(solution)/shard_map/ppermute | solution.py:25
  10.4 29.9 %collective-permute-start.9 = (bf16[256,512]{1,0:T(8,128)(2,1)}, bf16[256,512]{1,0:T(8,128)(2,1)S(1)}, u32[]{:S(2)}, u32[]{:S(2)}) collective-permute-start(bf16[256,512]{1,0:T(8,128)(2,1)} %v_ref.1), channel_id=1, source_target_pairs={{0,1},{1,0},{2,3},{3,2},{4,5},{5,4},{6,7},{7,6},{8,9},{9,8},{10,11... | collective-permute-start | bytes 786440 | tf_op jit(solution)/shard_map/ppermute | solution.py:25
  15.1 25.7 %collective-permute-start.11 = (bf16[256,512]{1,0:T(8,128)(2,1)S(1)}, bf16[256,512]{1,0:T(8,128)(2,1)S(1)}, u32[]{:S(2)}, u32[]{:S(2)}) collective-permute-start(bf16[256,512]{1,0:T(8,128)(2,1)S(1)} %collective-permute-done.10.refs_2_), channel_id=1, source_target_pairs={{0,1},{1,0},{2,3},{3,2},{4,5},{5,4},{6,7},{7,6},{8,9},{9,8},{10,11... | collective-permute-start | bytes 786440 | tf_op jit(solution)/shard_map/ppermute | solution.py:25
  15.1 1.5 %collective-permute-start.6 = (s32[1,256]{1,0:T(1,128)}, s32[1,256]{1,0:T(1,128)S(1)}, u32[]{:S(2)}, u32[]{:S(2)}) collective-permute-start(s32[1,256]{1,0:T(1,128)} %bitcast.1), channel_id=1, source_target_pairs={{0,1},{1,0},{2,3},{3,2},{4,5},{5,4},{6,7},{7,6},{8,9},{9,8},{10,11... | collective-permute-start | bytes 3080 | tf_op jit(solution)/shard_map/ppermute | solution.py:25
  16.7 3.8 %collective-permute-start.7 = (s32[1,256]{1,0:T(1,128)}, s32[1,256]{1,0:T(1,128)S(1)}, u32[]{:S(2)}, u32[]{:S(2)}) collective-permute-start(s32[1,256]{1,0:T(1,128)} %bitcast.2), channel_id=1, source_target_pairs={{0,2},{1,3},{2,0},{3,1},{4,6},{5,7},{6,4},{7,5},{8,10},{9,11},{10,... | collective-permute-start | bytes 3080 | tf_op jit(solution)/shard_map/ppermute | solution.py:25
  20.5 1.2 %collective-permute-start.8 = (s32[1,256]{1,0:T(1,128)S(1)}, s32[1,256]{1,0:T(1,128)S(1)}, u32[]{:S(2)}, u32[]{:S(2)}) collective-permute-start(s32[1,256]{1,0:T(1,128)S(1)} %collective-permute-done.7.refs_10_), channel_id=1, source_target_pairs={{0,1},{1,0},{2,3},{3,2},{4,5},{5,4},{6,7},{7,6},{8,9},{9,8},{10,11... | collective-permute-start | bytes 3080 | tf_op jit(solution)/shard_map/ppermute | solution.py:25
  21.6 4.7 %collective-permute-start = (bf16[8,4224]{1,0:T(8,128)(2,1)S(1)}, bf16[8,4224]{1,0:T(8,128)(2,1)S(1)}, u32[]{:S(2)}, u32[]{:S(2)}) collective-permute-start(bf16[8,4224]{1,0:T(8,128)(2,1)S(1)} %get-tuple-element.17.refs_0_), channel_id=1, source_target_pairs={{0,4},{1,5},{2,6},{3,7},{4,0},{5,1},{6,2},{7,3},{8,12},{9,13},{10,... | collective-permute-start | bytes 202760 | tf_op jit(solution)/shard_map/ppermute | solution.py:25
  26.3 6.5 %collective-permute-start.1 = (bf16[8,4224]{1,0:T(8,128)(2,1)S(1)}, bf16[8,4224]{1,0:T(8,128)(2,1)S(1)}, u32[]{:S(2)}, u32[]{:S(2)}) collective-permute-start(bf16[8,4224]{1,0:T(8,128)(2,1)S(1)} %get-tuple-element.17.refs_0_), channel_id=1, source_target_pairs={{0,8},{1,9},{2,10},{3,11},{4,12},{5,13},{6,14},{7,15},{8,0},{9,1},... | collective-permute-start | bytes 202760 | tf_op jit(solution)/shard_map/ppermute | solution.py:25
  32.8 6.1 %collective-permute-start.2 = (bf16[8,4224]{1,0:T(8,128)(2,1)S(1)}, bf16[8,4224]{1,0:T(8,128)(2,1)S(1)}, u32[]{:S(2)}, u32[]{:S(2)}) collective-permute-start(bf16[8,4224]{1,0:T(8,128)(2,1)S(1)} %get-tuple-element.17.refs_0_), channel_id=1, source_target_pairs={{0,12},{1,13},{2,14},{3,15},{4,8},{5,9},{6,10},{7,11},{8,4},{9,5},... | collective-permute-start | bytes 202760 | tf_op jit(solution)/shard_map/ppermute | solution.py:25
  41.2 4.7 %collective-permute-start.12 = (bf16[8,4224]{1,0:T(8,128)(2,1)S(1)}, bf16[8,4224]{1,0:T(8,128)(2,1)S(1)}, u32[]{:S(2)}, u32[]{:S(2)}) collective-permute-start(bf16[8,4224]{1,0:T(8,128)(2,1)S(1)} %get-tuple-element.24), channel_id=1, source_target_pairs={{0,4},{1,5},{2,6},{3,7},{4,0},{5,1},{6,2},{7,3},{8,12},{9,13},{10,... | collective-permute-start | bytes 202760 | tf_op jit(solution)/shard_map/ppermute | solution.py:25
  41.3 7.0 %collective-permute-start.13 = (bf16[8,4224]{1,0:T(8,128)(2,1)S(1)}, bf16[8,4224]{1,0:T(8,128)(2,1)S(1)}, u32[]{:S(2)}, u32[]{:S(2)}) collective-permute-start(bf16[8,4224]{1,0:T(8,128)(2,1)S(1)} %get-tuple-element.25), channel_id=1, source_target_pairs={{0,12},{1,13},{2,14},{3,15},{4,8},{5,9},{6,10},{7,11},{8,4},{9,5},... | collective-permute-start | bytes 202760 | tf_op jit(solution)/shard_map/ppermute | solution.py:25
  44.6 5.9 %collective-permute-start.14 = (bf16[8,4224]{1,0:T(8,128)(2,1)S(1)}, bf16[8,4224]{1,0:T(8,128)(2,1)S(1)}, u32[]{:S(2)}, u32[]{:S(2)}) collective-permute-start(bf16[8,4224]{1,0:T(8,128)(2,1)S(1)} %get-tuple-element.28), channel_id=1, source_target_pairs={{0,8},{1,9},{2,10},{3,11},{4,12},{5,13},{6,14},{7,15},{8,0},{9,1},... | collective-permute-start | bytes 202760 | tf_op jit(solution)/shard_map/ppermute | solution.py:25
